TPU v7x, 128 devices: a whole 4x4x4 slice. The times are simulated.
128 devices in a mesh: ctx: 32 (over x, y_lo, z), exp: 4 (over y_hi, core).
Axes of the slice: x: 4, y: 4 (y_hi: 2, y_lo: 2; y = y_hi * 2 + y_lo), z: 4, core: 2. Of those that a mesh axis runs over, the one named last changes fastest.
Arguments:
- residual: bfloat16 [4, 4096, 2048], P('exp', 'ctx'), may hold values from -6 to 6
- query_heads: bfloat16 [4, 4096, 2048], P('exp', 'ctx'), may hold values from -6.5 to 6.5
- key_heads: bfloat16 [4, 4096, 256], P('exp', 'ctx'), may hold values from -6 to 6
- value_heads: bfloat16 [4, 4096, 256], P('exp', 'ctx'), may hold values from -6 to 6
- norm_gain: float32 [2048], replicated, may hold values from 0.1 to 1.9
- chosen_experts: int32 [4, 4096, 8], P('exp', 'ctx'), may hold values from 0 to 127, all different within a row; in each aligned block of 128 rows (0 to 127, 128 to 255, ..., all dimensions but the last counted through in order) at most 9 rows name the same one
- route_weights: float32 [4, 4096, 8], P('exp', 'ctx'), may hold values from 0.05 to 1
- gate_weight: bfloat16 [128, 2048, 768], P(('ctx', 'exp')), may hold values from -0.125 to 0.125
- up_weight: bfloat16 [128, 2048, 768], P(('ctx', 'exp')), may hold values from -0.125 to 0.125
- down_weight: bfloat16 [128, 768, 2048], P(('ctx', 'exp')), may hold values from -0.21875 to 0.21875
- cotangent: bfloat16 [4, 4096, 2048], P('exp', 'ctx'), may hold values from -6 to 6
Outputs:
- layer_out: bfloat16 [4, 4096, 2048], P('exp', 'ctx')
- residual_gradient: bfloat16 [4, 4096, 2048], P('exp', 'ctx')
- query_gradient: bfloat16 [4, 4096, 2048], P('exp', 'ctx')
- key_gradient: bfloat16 [4, 4096, 256], P('exp', 'ctx')
- value_gradient: bfloat16 [4, 4096, 256], P('exp', 'ctx')
- route_gradient: float32 [4, 4096, 8], P('exp', 'ctx')
Inputs may be any that keep to these rules, and one draw needn't show every extreme that they name: `chosen_experts`: among the rows of one device no expert is named by more than 9 rows, a bound that some block reaches; the 8 experts of a row differ.
All inputs are finite; a program needn't handle non-finite values.
Results may differ from a plain program's by a relative error of at most 0.025.
Values may be sent and summed in bfloat16 or wider, within the bound.
A program may use at most 192 MiB of HBM per device.

v0:
```python
import jax
import jax.numpy as jnp
from jax import lax
from jax.sharding import PartitionSpec as P

H = 16
KVH = 2
DH = 128
TOPK = 8


NEG = -1e30
EPSILON = 1e-06


def place_rows(begin_row, row_count):
    row_index = begin_row + jnp.arange(row_count, dtype=jnp.int32)
    return row_index


def over_keys(key_local, value_local, visit, start_state):
    return visit(
        start_state,
        (
            lax.all_gather(key_local, "ctx", axis=0, tiled=True),
            lax.all_gather(value_local, "ctx", axis=0, tiled=True),
        ),
        jnp.int32(0),
    )


def to_experts(rows_out):
    return lax.all_to_all(rows_out, ("ctx", "exp"), split_axis=0, concat_axis=0, tiled=True)


def from_experts(rows_back):
    return lax.all_to_all(rows_back, ("ctx", "exp"), split_axis=0, concat_axis=0, tiled=True)


def forward_tile(state, query_half, query_place, key_block, value_block, key_place, score_scale):
    run_max, run_sum, run_acc = state
    scores = (
        jnp.einsum("ikgd,jkd->kgij", query_half, key_block, preferred_element_type=jnp.float32)
        * score_scale
    )
    allowed = key_place[None, :] <= query_place[:, None]
    scores = jnp.where(allowed, scores, NEG)
    new_max = jnp.maximum(run_max, jnp.max(scores, axis=-1))
    weights = jnp.where(allowed, jnp.exp(scores - new_max[..., None]), 0.0)
    run_sum = jnp.sum(weights, axis=-1)
    run_acc = jnp.einsum(
        "kgij,jkd->kgid",
        weights.astype(jnp.bfloat16),
        value_block,
        preferred_element_type=jnp.float32,
    )
    return (new_max, run_sum, run_acc)


def backward_tile(
    query_acc,
    query_half,
    query_place,
    grad_half,
    log_half,
    dot_half,
    key_block,
    value_block,
    key_place,
    score_scale,
):
    scores = (
        jnp.einsum("ikgd,jkd->kgij", query_half, key_block, preferred_element_type=jnp.float32)
        * score_scale
    )
    allowed = key_place[None, :] <= query_place[:, None]
    weights = jnp.where(allowed, jnp.exp(scores - log_half[..., None]), 0.0)
    value_part = jnp.einsum(
        "kgij,ikgd->jkd",
        weights.astype(jnp.bfloat16),
        grad_half,
        preferred_element_type=jnp.float32,
    )
    grad_weights = jnp.einsum(
        "ikgd,jkd->kgij", grad_half, value_block, preferred_element_type=jnp.float32
    )
    grad_scores = (weights * (grad_weights - dot_half[..., None])).astype(jnp.bfloat16)
    query_acc = (
        jnp.einsum("kgij,jkd->kgid", grad_scores, key_block, preferred_element_type=jnp.float32)
        * score_scale
    )
    key_part = (
        jnp.einsum("kgij,ikgd->jkd", grad_scores, query_half, preferred_element_type=jnp.float32)
        * score_scale
    )
    return (query_acc, key_part, value_part)


def per_device(
    residual,
    query_heads,
    key_heads,
    value_heads,
    norm_gain,
    chosen_experts,
    route_weights,
    gate_weight,
    up_weight,
    down_weight,
    cotangent,
):
    shard_rows = residual.shape[1]
    width = residual.shape[2]
    kv_width = key_heads.shape[2]
    query_width = query_heads.shape[2]
    group_size = H // KVH
    half_rows = shard_rows // 2
    ctx_count = lax.axis_size("ctx")
    seq_rows = shard_rows * ctx_count
    score_scale = DH ** (-0.5)
    ctx_index = lax.axis_index("ctx")
    packed = jnp.concatenate([query_heads[0], key_heads[0], value_heads[0]], axis=1)
    query_local = packed[:, :query_width].reshape(shard_rows, KVH, group_size, DH)
    key_local = packed[:, query_width : query_width + kv_width]
    value_local = packed[:, query_width + kv_width :]
    query_place = place_rows(ctx_index * shard_rows, shard_rows)

    def forward_visit(state, piece, begin_row):
        key_rows, value_rows = piece
        row_count = key_rows.shape[0]
        key_block = key_rows.reshape(row_count, KVH, DH)
        value_block = value_rows.reshape(row_count, KVH, DH)
        key_place = place_rows(begin_row, row_count)
        updated = []
        for which_half in range(2):
            query_half = query_local[which_half * half_rows : (which_half + 1) * half_rows]
            place_half = query_place[which_half * half_rows : (which_half + 1) * half_rows]
            updated.append(
                lax.cond(
                    jnp.min(key_place) <= jnp.max(place_half),
                    lambda inner: forward_tile(
                        inner,
                        query_half,
                        place_half,
                        key_block,
                        value_block,
                        key_place,
                        score_scale,
                    ),
                    lambda inner: inner,
                    state[which_half],
                )
            )
        return tuple(updated)

    start_half = (
        jnp.full((KVH, group_size, half_rows), NEG, jnp.float32),
        jnp.zeros((KVH, group_size, half_rows), jnp.float32),
        jnp.zeros((KVH, group_size, half_rows, DH), jnp.float32),
    )
    halves = over_keys(key_local, value_local, forward_visit, (start_half, start_half))
    attended = jnp.concatenate(
        [acc_half / sum_half[..., None] for max_half, sum_half, acc_half in halves], axis=2
    )
    log_sum = jnp.concatenate(
        [max_half + jnp.log(sum_half) for max_half, sum_half, acc_half in halves], axis=2
    )
    attended_local = (
        jnp.transpose(attended, (2, 0, 1, 3)).reshape(shard_rows, query_width).astype(jnp.bfloat16)
    )
    hidden = (residual[0].astype(jnp.float32) + attended_local.astype(jnp.float32)).astype(
        jnp.bfloat16
    )
    hidden_float = hidden.astype(jnp.float32)
    inverse = lax.rsqrt(jnp.mean(hidden_float * hidden_float, axis=-1, keepdims=True) + EPSILON)
    normed = (hidden_float * inverse * norm_gain).astype(jnp.bfloat16)
    expert_count = ctx_count * lax.axis_size("exp")
    capacity = (9 * shard_rows * TOPK + 8 * expert_count - 1) // (8 * expert_count)
    chosen_flat = chosen_experts[0].reshape(-1)
    onehot_hits = (
        chosen_flat[:, None] == jnp.arange(expert_count, dtype=jnp.int32)[None, :]
    ).astype(jnp.int32)
    earlier = jnp.cumsum(onehot_hits, axis=0) - onehot_hits
    slot_index = jnp.sum(earlier * onehot_hits, axis=1)
    target = chosen_flat * capacity + slot_index
    share_raw = route_weights[0]
    route_total = jnp.sum(share_raw, axis=-1, keepdims=True)
    route_share = share_raw / route_total
    cot_float = cotangent[0].astype(jnp.float32)

    def spread(row_values):
        filled = (
            jnp.zeros((expert_count * capacity, width), jnp.bfloat16).at[target].set(row_values)
        )
        return filled.reshape(expert_count, capacity, width)

    gate_mat = gate_weight[0]
    up_mat = up_weight[0]
    down_mat = down_weight[0]
    incoming = to_experts(spread(jnp.repeat(normed, TOPK, axis=0))).reshape(-1, width)
    gate_act = jnp.dot(incoming, gate_mat, preferred_element_type=jnp.float32)
    up_act = jnp.dot(incoming, up_mat, preferred_element_type=jnp.float32)
    activation = (jax.nn.silu(gate_act) * up_act).astype(jnp.bfloat16)
    produced = jnp.dot(activation, down_mat, preferred_element_type=jnp.float32).astype(
        jnp.bfloat16
    )
    returned = from_experts(produced.reshape(expert_count, capacity, width)).reshape(-1, width)
    picked = returned[target].reshape(shard_rows, TOPK, width)
    moe_sum = jnp.sum(route_share[:, :, None] * picked.astype(jnp.float32), axis=1)
    layer_out = (hidden_float + moe_sum).astype(jnp.bfloat16)
    route_dot = jnp.sum(picked.astype(jnp.float32) * cot_float[:, None, :], axis=-1)
    route_gradient = (
        route_dot - jnp.sum(route_share * route_dot, axis=-1, keepdims=True)
    ) / route_total
    out_cot = (
        (route_share[:, :, None] * cot_float[:, None, :]).astype(jnp.bfloat16).reshape(-1, width)
    )
    cot_in = to_experts(spread(out_cot)).reshape(-1, width)
    act_cot = lax.dot_general(
        cot_in, down_mat, (((1,), (1,)), ((), ())), preferred_element_type=jnp.float32
    )
    sigma_gate = jax.nn.sigmoid(gate_act)
    gate_cot = (act_cot * up_act * sigma_gate * (1.0 + gate_act * (1.0 - sigma_gate))).astype(
        jnp.bfloat16
    )
    up_cot = (act_cot * gate_act * sigma_gate).astype(jnp.bfloat16)
    row_cot = (
        lax.dot_general(
            gate_cot, gate_mat, (((1,), (1,)), ((), ())), preferred_element_type=jnp.float32
        )
        + lax.dot_general(
            up_cot, up_mat, (((1,), (1,)), ((), ())), preferred_element_type=jnp.float32
        )
    ).astype(jnp.bfloat16)
    cot_back = from_experts(row_cot.reshape(expert_count, capacity, width)).reshape(-1, width)
    normed_cot = jnp.sum(
        cot_back[target].reshape(shard_rows, TOPK, width).astype(jnp.float32), axis=1
    )
    gained = norm_gain * normed_cot
    hidden_cot = inverse * gained - hidden_float * inverse**3 * jnp.mean(
        hidden_float * gained, axis=-1, keepdims=True
    )
    residual_gradient = (cot_float + hidden_cot).astype(jnp.bfloat16)
    grad_local = residual_gradient.reshape(shard_rows, KVH, group_size, DH)
    attended_rows = attended_local.reshape(shard_rows, KVH, group_size, DH)
    row_dot = jnp.einsum(
        "ikgd,ikgd->kgi", grad_local, attended_rows, preferred_element_type=jnp.float32
    )

    def backward_visit(state, piece, begin_row):
        query_accs, key_total, value_total = state
        key_rows, value_rows = piece
        row_count = key_rows.shape[0]
        key_block = key_rows.reshape(row_count, KVH, DH)
        value_block = value_rows.reshape(row_count, KVH, DH)
        key_place = place_rows(begin_row, row_count)
        empty_block = jnp.zeros((row_count, KVH, DH), jnp.float32)
        key_sum = empty_block
        value_sum = empty_block
        new_accs = []
        for which_half in range(2):
            lower = which_half * half_rows
            upper = lower + half_rows
            query_half = query_local[lower:upper]
            place_half = query_place[lower:upper]
            grad_half = grad_local[lower:upper]
            log_half = log_sum[:, :, lower:upper]
            dot_half = row_dot[:, :, lower:upper]
            query_acc, key_part, value_part = lax.cond(
                jnp.min(key_place) <= jnp.max(place_half),
                lambda inner: backward_tile(
                    inner,
                    query_half,
                    place_half,
                    grad_half,
                    log_half,
                    dot_half,
                    key_block,
                    value_block,
                    key_place,
                    score_scale,
                ),
                lambda inner: (inner, empty_block, empty_block),
                query_accs[which_half],
            )
            new_accs.append(query_acc)
            key_sum = key_sum + key_part
            value_sum = value_sum + value_part
        key_total = key_sum.reshape(row_count, -1)
        value_total = value_sum.reshape(row_count, -1)
        return (tuple(new_accs), key_total, value_total)

    empty_query = jnp.zeros((KVH, group_size, half_rows, DH), jnp.float32)
    empty_keys = jnp.zeros((seq_rows, kv_width), jnp.float32)
    query_accs, key_total, value_total = over_keys(
        key_local, value_local, backward_visit, ((empty_query, empty_query), empty_keys, empty_keys)
    )
    key_own, value_own = (
        lax.psum_scatter(
            key_total.astype(jnp.bfloat16), "ctx", scatter_dimension=0, tiled=True
        ).astype(jnp.float32),
        lax.psum_scatter(
            value_total.astype(jnp.bfloat16), "ctx", scatter_dimension=0, tiled=True
        ).astype(jnp.float32),
    )
    query_grad = jnp.transpose(jnp.concatenate(query_accs, axis=2), (2, 0, 1, 3)).reshape(
        shard_rows, query_width
    )
    grads_packed = jnp.concatenate(
        [
            query_grad.astype(jnp.bfloat16),
            key_own.astype(jnp.bfloat16),
            value_own.astype(jnp.bfloat16),
        ],
        axis=1,
    )
    query_gradient = grads_packed[:, :query_width]
    key_gradient = grads_packed[:, query_width : query_width + kv_width]
    value_gradient = grads_packed[:, query_width + kv_width :]
    return (
        layer_out[None],
        residual_gradient[None],
        query_gradient[None],
        key_gradient[None],
        value_gradient[None],
        route_gradient[None],
    )


def solution(mesh):
    in_specs = (
        P("exp", "ctx", None),
        P("exp", "ctx", None),
        P("exp", "ctx", None),
        P("exp", "ctx", None),
        P(),
        P("exp", "ctx", None),
        P("exp", "ctx", None),
        P(("ctx", "exp"), None, None),
        P(("ctx", "exp"), None, None),
        P(("ctx", "exp"), None, None),
        P("exp", "ctx", None),
    )
    out_specs = (
        P("exp", "ctx", None),
        P("exp", "ctx", None),
        P("exp", "ctx", None),
        P("exp", "ctx", None),
        P("exp", "ctx", None),
        P("exp", "ctx", None),
    )
    return jax.shard_map(
        per_device, mesh=mesh, in_specs=in_specs, out_specs=out_specs, check_vma=False
    )
```

profile of v0, /device:TPU:0, one launch (start us, length us, event | category | flops | bytes accessed | tf_op | source)
XLA Modules:
  0.0 1245.4 jit_solution(13929531508248828289)
XLA Ops:
  7.2 1.7 copy.64
  9.0 1.6 copy.65
  17.2 2.6 convert_bitcast_fusion
  19.8 10.2 scatter_custom_fusion.1
  29.9 8.1 reshape.375
  38.1 11.7 all-to-all-start.2
  53.6 173.6 %all-gather.5.cloned.1.call-done = bf16[1,4096,256]{1,2,0:T(8,128)(2,1)} async-done(((bf16[1,128,256]{1,2,0:T(8,128)(2,1)}), bf16[1,4096,256]{1,2,0:T(8,128)(2,1)}) %all-gather.5.cloned.1.call-update) | async-done | bytes 2097168 | tf_op jit(solution)/shard_map/all_gather | solution.py:25
  227.2 126.3 %all-gather.7.cloned.1.call-done = bf16[1,4096,256]{1,2,0:T(8,128)(2,1)} async-done(((bf16[1,128,256]{1,2,0:T(8,128)(2,1)}), bf16[1,4096,256]{1,2,0:T(8,128)(2,1)}) %all-gather.7.cloned.1.call-update) | async-done | bytes 2097168 | tf_op jit(solution)/shard_map/all_gather | solution.py:26
  353.5 28.2 %conditional.5 = (f32[2,8,64]{2,1,0:T(8,128)}, f32[2,8,64]{2,1,0:T(8,128)}, f32[2,8,64,128]{3,2,1,0:T(8,128)S(1)}, f32[2,8,64]{2,1,0:T(8,128)S(1)}) conditional(s32[]{:T(128)} %convert_element_type.216, () %tuple.46, (s32[4096]{0:T(1024)S(1)}, s32[64]{0:T(128)S(1)}, bf16[4096,2,128]{0,2,1:T(8,128)(2,1)}, bf16[64,2,8,128]{3,2,1,0:T(8,128)(2,1)S(1)}, ...), branch_computations={%region_6.7_spmd, %region_7.10_spmd} | conditional | flops 2202270720 | bytes 56410400 | solution.py:139
  353.9 9.0 fusion.13
  363.5 8.2 fusion.16
  371.8 9.2 fusion.15
  382.5 29.6 %conditional.4 = (f32[2,8,64]{2,1,0:T(8,128)}, f32[2,8,64]{2,1,0:T(8,128)}, f32[2,8,64,128]{3,2,1,0:T(8,128)S(1)}, f32[2,8,64]{2,1,0:T(8,128)S(1)}) conditional(s32[]{:T(128)} %convert_element_type.215, () %tuple.44, (s32[4096]{0:T(1024)S(1)}, s32[64]{0:T(128)S(1)}, bf16[4096,2,128]{0,2,1:T(8,128)(2,1)}, bf16[64,2,8,128]{3,2,1,0:T(8,128)(2,1)}, ...), branch_computations={%region_1.0_spmd, %region_2.5_spmd} | conditional | flops 2202270720 | bytes 56410400 | solution.py:139
  382.7 10.2 fusion
  393.5 8.2 fusion.3
  401.8 9.2 fusion.2
  412.1 1.5 broadcast_divide_fusion
  417.7 9.9 scatter_custom_fusion
  427.6 8.1 reshape.371
  435.7 8.8 all-to-all-start
  444.5 8.4 reshape.376
  453.0 8.9 fusion.95
  461.9 90.1 %all-to-all-done = bf16[128,9,2048]{2,1,0:T(8,128)(2,1)} async-done(((bf16[128,9,2048]{2,1,0:T(8,128)(2,1)}), bf16[128,9,2048]{2,1,0:T(8,128)(2,1)}, u32[]{:S(2)}, u32[]{:S(2)}) %all-to-all-start) | async-done | bytes 4718624 | tf_op jit(solution)/shard_map/all_to_all | solution.py:33
  552.0 8.5 reshape.372
  560.5 5.9 fusion.103
  566.4 3.9 fusion.99
  570.3 1.7 copy-done.38
  572.1 8.3 fusion.101
  580.3 8.3 add_convert_fusion
  588.6 8.1 reshape.377
  596.7 11.1 all-to-all-start.3
  608.0 1.2 copy.138
  609.2 1.2 copy.136
  610.4 106.7 %all-to-all-done.3 = bf16[128,9,2048]{2,1,0:T(8,128)(2,1)} async-done(((bf16[128,9,2048]{2,1,0:T(8,128)(2,1)}), bf16[128,9,2048]{2,1,0:T(8,128)(2,1)}, u32[]{:S(2)}, u32[]{:S(2)}) %all-to-all-start.3) | async-done | bytes 4718624 | tf_op jit(solution)/shard_map/all_to_all | solution.py:37
  717.1 8.4 reshape.378
  725.5 11.8 gather_fusion.1
  737.3 5.2 convert_reduce_fusion
  743.6 1.2 fusion.128
  744.8 39.8 %conditional.6 = (f32[4096,2,128]{2,0,1:T(8,128)}, f32[4096,2,128]{2,0,1:T(8,128)}, bf16[2,8,64,128]{3,2,1,0:T(8,128)(2,1)S(1)}) conditional(s32[]{:T(128)} %convert_element_type.215, () %tuple.48, (s32[4096]{0:T(1024)S(1)}, s32[64]{0:T(128)S(1)}, bf16[4096,2,128]{0,2,1:T(8,128)(2,1)S(1)}, bf16[64,2,8,128]{3,2,1,0:T(8,128)(2,1)S(1)}, ...), branch_computations={%region_20.21_spmd, %region_21.22_spmd} | conditional | flops 5412226048 | bytes 95461712 | solution.py:269
  746.3 8.1 fusion.42
  754.4 12.9 %fusion.34 = f32[4096,2,128]{2,0,1:T(8,128)} fusion(f32[2,4096,64,8]{1,2,3,0:T(8,128)} %fusion.42, f32[2,8,64]{2,1,0:T(8,128)S(1)} %add.75, pred[64,4096]{1,0:T(8,128)(4,1)S(1)} %broadcast_compare_fusion.2, bf16[64,2,8,128]{3,2,1,0:T(8,128)(2,1)S(1)} %bitcast.303), kind=kOutput, calls=%fused_computation.45 | convolution fusion | flops 1090519040 | bytes 21499904 | tf_op jit(solution)/shard_map/cond/branch_1_fun/kgij,ikgd->jkd/dot_general | solution.py:78
  767.3 9.5 fusion.27
  776.8 2.3 fusion.47
  779.1 5.3 fusion.38
  785.4 40.5 %conditional.7 = (f32[4096,2,128]{2,0,1:T(8,128)}, f32[4096,2,128]{2,0,1:T(8,128)}, bf16[2,8,64,128]{3,2,1,0:T(8,128)(2,1)S(1)}) conditional(s32[]{:T(128)} %convert_element_type.216, () %tuple.50, (s32[4096]{0:T(1024)S(1)}, s32[64]{0:T(128)S(1)}, bf16[4096,2,128]{0,2,1:T(8,128)(2,1)S(1)}, bf16[64,2,8,128]{3,2,1,0:T(8,128)(2,1)S(1)}, ...), branch_computations={%region_22.23_spmd, %region_23.24_spmd} | conditional | flops 5412226048 | bytes 93372696 | solution.py:269
  787.4 8.1 fusion.72
  795.4 12.9 %fusion.64 = f32[4096,2,128]{2,0,1:T(8,128)} fusion(f32[2,4096,64,8]{1,2,3,0:T(8,128)} %fusion.72, f32[2,8,64]{2,1,0:T(8,128)S(1)} %add.76, pred[64,4096]{1,0:T(8,128)(4,1)S(1)} %broadcast_compare_fusion.3, bf16[64,2,8,128]{3,2,1,0:T(8,128)(2,1)S(1)} %bitcast.301), kind=kOutput, calls=%fused_computation.73 | convolution fusion | flops 1090519040 | bytes 21499904 | tf_op jit(solution)/shard_map/cond/branch_1_fun/kgij,ikgd->jkd/dot_general | solution.py:78
  808.3 9.6 fusion.57
  817.9 2.3 fusion.77
  820.2 5.3 fusion.68
  825.9 5.3 copy_bitcast_fusion.1
  831.2 10.0 convolution_convert_fusion
  841.2 8.1 reshape.373
  849.4 10.3 all-to-all-start.1
  859.7 5.3 copy_bitcast_fusion
  865.2 1.1 reshape.379
  866.3 100.4 %all-to-all-done.1 = bf16[128,9,2048]{2,1,0:T(8,128)(2,1)} async-done(((bf16[128,9,2048]{2,1,0:T(8,128)(2,1)}), bf16[128,9,2048]{2,1,0:T(8,128)(2,1)}, u32[]{:S(2)}, u32[]{:S(2)}) %all-to-all-start.1) | async-done | bytes 4718624 | tf_op jit(solution)/shard_map/all_to_all | solution.py:37
  966.8 8.4 reshape.374
  975.2 11.8 gather_fusion
  987.0 6.1 fusion.87
  996.2 2.1 convert_element_type.257
  998.2 3.6 fusion.119
  1001.8 73.6 %reduce-scatter.3.cloned.1.call-done = bf16[128,256]{1,0:T(8,128)(2,1)} async-done(((bf16[4096,256]{1,0:T(8,128)(2,1)}), bf16[128,256]{1,0:T(8,128)(2,1)}) %reduce-scatter.3.cloned.1.call-update) | async-done | bytes 65552 | tf_op jit(solution)/shard_map/reduce_scatter | solution.py:299
  1075.4 162.9 %reduce-scatter.5.cloned.1.call-done = bf16[128,256]{1,0:T(8,128)(2,1)} async-done(((bf16[4096,256]{1,0:T(8,128)(2,1)}), bf16[128,256]{1,0:T(8,128)(2,1)}) %reduce-scatter.5.cloned.1.call-update) | async-done | bytes 65552 | tf_op jit(solution)/shard_map/reduce_scatter | solution.py:302
  (148 shorter events, 25.2 us)
Async XLA Ops:
  7.2 553.3 %copy-start = (bf16[1,2048,768]{2,1,0:T(8,128)(2,1)S(1)}, bf16[1,2048,768]{2,1,0:T(8,128)(2,1)}, u32[]{:S(2)}) copy-start(bf16[1,2048,768]{2,1,0:T(8,128)(2,1)} %param.26) | copy-start | bytes 9437188
  7.2 220.0 %all-gather.5.cloned.1.call-start = ((), (), s32[]{:S(2)}) async-start(), calls=%async_computation.8 | async-start | bytes 2162688 | tf_op jit(solution)/shard_map/all_gather | solution.py:25
  9.0 344.5 %all-gather.7.cloned.1.call-start = ((), (), s32[]{:S(2)}) async-start(), calls=%async_computation.9 | async-start | bytes 2162688 | tf_op jit(solution)/shard_map/all_gather | solution.py:26
  13.1 16.9 %copy-start.25 = (f32[1,128,8]{2,1,0:T(8,128)}, f32[1,128,8]{2,1,0:T(8,128)S(1)}, u32[]{:S(2)}) copy-start(f32[1,128,8]{2,1,0:T(8,128)S(1)} %copy.73) | copy-start | bytes 12292
  13.8 0.6 copy-start.31
  14.8 0.8 copy-start.22
  38.1 397.6 %all-to-all-start.2 = ((bf16[128,9,2048]{2,1,0:T(8,128)(2,1)}), bf16[128,9,2048]{2,1,0:T(8,128)(2,1)}, u32[]{:S(2)}, u32[]{:S(2)}) async-start(bf16[128,9,2048]{2,1,0:T(8,128)(2,1)} %reshape.375), calls=%async_computation.2 | async-start | bytes 16777216 | tf_op jit(solution)/shard_map/all_to_all | solution.py:33
  381.7 0.8 copy-start.23
  412.1 3.3 copy-start.9
  412.1 4.6 copy-start.30
  413.6 0.7 copy-start.18
  413.6 0.8 copy-start.20
  414.4 1.0 copy-start.4
  415.9 0.8 copy-start.6
  416.0 327.6 %copy-start.33 = (f32[128]{0:T(128)}, f32[128]{0:T(128)S(1)}, u32[]{:S(2)}) copy-start(f32[128]{0:T(128)S(1)} %get-tuple-element.208) | copy-start | bytes 1540
  435.7 116.3 %all-to-all-start = ((bf16[128,9,2048]{2,1,0:T(8,128)(2,1)}), bf16[128,9,2048]{2,1,0:T(8,128)(2,1)}, u32[]{:S(2)}, u32[]{:S(2)}) async-start(bf16[128,9,2048]{2,1,0:T(8,128)(2,1)} %reshape.371), calls=%async_computation | async-start | bytes 16777216 | tf_op jit(solution)/shard_map/all_to_all | solution.py:33
  560.5 5.9 copy-start.8
  560.5 5.9 copy-start.35
  566.4 13.9 %copy-start.36 = (f32[1152,768]{1,0:T(8,128)}, f32[1152,768]{1,0:T(8,128)S(1)}, u32[]{:S(2)}) copy-start(f32[1152,768]{1,0:T(8,128)S(1)} %fusion.103) | copy-start | bytes 10616836
  566.4 5.6 copy-start.37
  570.3 1.8 copy-start.38
  596.7 11.2 copy-start.10
  596.7 12.4 copy-start.14
  596.7 120.4 %all-to-all-start.3 = ((bf16[128,9,2048]{2,1,0:T(8,128)(2,1)}), bf16[128,9,2048]{2,1,0:T(8,128)(2,1)}, u32[]{:S(2)}, u32[]{:S(2)}) async-start(bf16[128,9,2048]{2,1,0:T(8,128)(2,1)} %reshape.377), calls=%async_computation.3 | async-start | bytes 16777216 | tf_op jit(solution)/shard_map/all_to_all | solution.py:37
  607.8 467.6 %reduce-scatter.3.cloned.1.call-start = ((), (), s32[]{:S(2)}) async-start(), calls=%async_computation.6 | async-start | bytes 2162688 | tf_op jit(solution)/shard_map/reduce_scatter | solution.py:299
  737.3 5.2 copy-start.7
  737.3 5.7 copy-start.11
  737.3 6.3 copy-start.12
  737.3 6.3 copy-start.13
  737.3 6.3 copy-start.19
  737.3 6.3 copy-start.21
  742.5 2.3 copy-start.3
  742.5 2.3 copy-start.2
  742.5 2.3 copy-start.15
  742.8 2.0 copy-start.34
  743.6 1.3 copy-start.24
  745.3 1.0 copy-start.16
  776.8 2.4 copy-start.17
  784.6 0.7 copy-start.27
  825.9 5.3 copy-start.29
  849.4 117.4 %all-to-all-start.1 = ((bf16[128,9,2048]{2,1,0:T(8,128)(2,1)}), bf16[128,9,2048]{2,1,0:T(8,128)(2,1)}, u32[]{:S(2)}, u32[]{:S(2)}) async-start(bf16[128,9,2048]{2,1,0:T(8,128)(2,1)} %reshape.373), calls=%async_computation.1 | async-start | bytes 16777216 | tf_op jit(solution)/shard_map/all_to_all | solution.py:37
  859.6 378.7 %reduce-scatter.5.cloned.1.call-start = ((), (), s32[]{:S(2)}) async-start(), calls=%async_computation.7 | async-start | bytes 2162688 | tf_op jit(solution)/shard_map/reduce_scatter | solution.py:302
  859.7 5.4 copy-start.26
  859.7 5.4 copy-start.32
  859.7 5.5 copy-start.5
  987.0 7.0 copy-start.28
  987.0 251.3 %copy-start.1 = (bf16[1,2048,768]{2,1,0:T(8,128)(2,1)S(1)}, bf16[1,2048,768]{2,1,0:T(8,128)(2,1)}, u32[]{:S(2)}) copy-start(bf16[1,2048,768]{2,1,0:T(8,128)(2,1)} %param.26) | copy-start | bytes 9437188
Sparse Core Ops, SparseCore 0:
  10.2 217.0 all-gather.4
  229.4 124.1 all-gather.6
  831.3 244.0 reduce-scatter.2
  1078.3 159.9 reduce-scatter.4
where the time goes:
time: 1250 us
  waiting for transfers between devices  834 us (67%)
  matrix products  157 us (13%)
  local copies, waits for them, and re-layouts  124 us (10%)
  other arithmetic  70.5 us (6%)
  starting transfers between devices  42 us (3%)
  between operations  16.2 us (1%)
    all_to_all x2, waiting for transfers between devices, from_experts(): lax.all_to_all(rows_back, ('ctx', 'exp'), split_axis=0, concat_axis=0, ti...  207 us
    all_gather x1, waiting for transfers between devices, over_keys(): lax.all_gather(key_local, 'ctx', axis=0, tiled=True)  174 us
    reduce_scatter x1, waiting for transfers between devices, per_device(): lax.psum_scatter(value_total.astype(jnp.bfloat16), 'ctx', scatter_dimensi...  163 us
    all_gather x1, waiting for transfers between devices, over_keys(): lax.all_gather(value_local, 'ctx', axis=0, tiled=True)  126 us
    all_to_all x2, waiting for transfers between devices, to_experts(): lax.all_to_all(rows_out, ('ctx', 'exp'), split_axis=0, concat_axis=0, til...  90.1 us
    reduce_scatter x1, waiting for transfers between devices, per_device(): lax.psum_scatter(key_total.astype(jnp.bfloat16), 'ctx', scatter_dimension...  73.6 us
    dot_general x2, matrix products, backward_tile(): jnp.einsum('kgij,ikgd->jkd', weights.astype(jnp.bfloat16), grad_half, pre...  25.8 us
  transfers between devices with their start and end apart: 8, of which 7 were waited for; matrix products, arithmetic and copies ran while one was open for 15% of the time, Pallas kernels for 0%

commit v1 on v0

v1 whole, which is shorter than its diff:
```python
import functools
import math

import jax
import jax.numpy as jnp
from jax import lax
from jax.experimental import pallas as pl
from jax.experimental.pallas import tpu as pltpu
from jax.sharding import PartitionSpec as P

H = 16
KVH = 2
DH = 128
TOPK = 8
GROUP = H // KVH
GQ = GROUP * DH

NEG = -1e30
EPSILON = 1e-06
SCALE = DH ** (-0.5)
SCALE2 = SCALE * math.log2(math.e)
SLOTS = 8
EXTRA = 256
KEY_BLOCK = 256
VMEM_LIMIT = 60 * 1024 * 1024

HIGHEST = lax.Precision.HIGHEST
NN = (((1,), (0,)), ((), ()))
NT = (((1,), (1,)), ((), ()))


def iota(shape, dim):
    return lax.broadcasted_iota(jnp.int32, shape, dim)


def dot(a, b, dims=NN, precision=None):
    return lax.dot_general(a, b, dims, precision=precision, preferred_element_type=jnp.float32)


def call(kernel, out_shape, args, flops=0, **kwargs):
    moved = sum(math.prod(a.shape) * a.dtype.itemsize for a in args)
    leaves = out_shape if isinstance(out_shape, (tuple, list)) else (out_shape,)
    moved += sum(math.prod(a.shape) * a.dtype.itemsize for a in leaves)
    return pl.pallas_call(
        kernel,
        out_shape=out_shape,
        compiler_params=pltpu.CompilerParams(vmem_limit_bytes=VMEM_LIMIT),
        cost_estimate=pl.CostEstimate(flops=flops, bytes_accessed=moved, transcendentals=0),
        **kwargs,
    )(*args)


def shape(dims, dtype):
    return jax.ShapeDtypeStruct(dims, dtype)


def repeat_rows(experts):
    dims = (experts * SLOTS, experts)
    return lax.shift_right_logical(iota(dims, 0), 3) == iota(dims, 1)


def repeat_lanes(experts):
    dims = (experts, experts * SLOTS)
    return iota(dims, 0) == lax.shift_right_logical(iota(dims, 1), 3)


def one(mask):
    return jnp.where(mask, 1.0, 0.0)


def low(mask):
    return one(mask).astype(jnp.bfloat16)


def spread_rows(rows_ref, slot_by_expert, send_ref, share_by_expert=None):
    experts, tokens = slot_by_expert.shape
    width = rows_ref.shape[1]
    total = experts * SLOTS
    repeat = repeat_rows(experts)
    slot = dot(low(repeat), slot_by_expert.astype(jnp.bfloat16))
    place = jnp.bitwise_and(iota((total, tokens), 0), SLOTS - 1)
    first = slot == place.astype(jnp.float32)
    ninth = slot == float(SLOTS)
    if share_by_expert is not None:
        share = dot(one(repeat), share_by_expert, precision=HIGHEST)
        first_share = jnp.sum(jnp.where(first, share, 0.0), axis=1, keepdims=True)
        ninth_share = jnp.sum(jnp.where(ninth, share, 0.0), axis=1, keepdims=True)
    pick = low(first)
    for c in range(width // EXTRA):
        part = dot(pick, rows_ref[:, c * EXTRA : (c + 1) * EXTRA])
        if share_by_expert is not None:
            part = part * first_share
        send_ref[:, c * EXTRA : (c + 1) * EXTRA] = part.astype(jnp.bfloat16)
    fold = jnp.concatenate([low(ninth & (place == r)) for r in range(SLOTS)], axis=1)
    folded = jnp.concatenate(
        [rows_ref[:, r * EXTRA : (r + 1) * EXTRA] for r in range(SLOTS)], axis=0
    )
    part = dot(fold, folded)
    if share_by_expert is not None:
        part = part * ninth_share
    send_ref[:, width:] = part.astype(jnp.bfloat16)


def send_cot_kernel(chosen_ref, route_ref, cot_ref, send_ref, slot_ref, slot_t_ref, share_ref):
    tokens = chosen_ref.shape[0]
    experts = slot_ref.shape[1]
    chosen = chosen_ref[...]
    route = route_ref[...]
    share_raw = route / jnp.sum(route, axis=1, keepdims=True)
    lanes = iota((tokens, experts), 1)
    hit = jnp.zeros((tokens, experts), jnp.float32)
    share = jnp.zeros((tokens, experts), jnp.float32)
    for k in range(TOPK):
        match = chosen[:, k : k + 1] == lanes
        hit = jnp.where(match, 1.0, hit)
        share = jnp.where(match, share_raw[:, k : k + 1], share)
    earlier = low(iota((tokens, tokens), 1) < iota((tokens, tokens), 0))
    slot = jnp.where(hit > 0.0, dot(earlier, hit.astype(jnp.bfloat16)), -1.0)
    slot_t = slot.T
    slot_ref[...] = slot
    slot_t_ref[...] = slot_t
    share_ref[...] = share
    spread_rows(cot_ref, slot_t, send_ref, share.T)


def send_normed_kernel(residual_ref, attended_ref, gain_ref, slot_t_ref, send_ref, hidden_ref, normed_ref):
    hidden = (residual_ref[...].astype(jnp.float32) + attended_ref[...].astype(jnp.float32)).astype(
        jnp.bfloat16
    )
    hidden_ref[...] = hidden
    hidden_float = hidden.astype(jnp.float32)
    inverse = lax.rsqrt(jnp.mean(hidden_float * hidden_float, axis=1, keepdims=True) + EPSILON)
    normed_ref[...] = (hidden_float * inverse * gain_ref[...]).astype(jnp.bfloat16)
    spread_rows(normed_ref, slot_t_ref[...], send_ref)


def unfold_ninth(rows_ref, ninth_ref):
    sources, width = ninth_ref.shape
    dims = (sources, sources * SLOTS)
    own = iota(dims, 0) == lax.shift_right_logical(iota(dims, 1), 3)
    place = jnp.bitwise_and(iota(dims, 1), SLOTS - 1)
    for r in range(SLOTS):
        ninth_ref[:, r * EXTRA : (r + 1) * EXTRA] = dot(
            low(own & (place == r)), rows_ref[:, width:]
        ).astype(jnp.bfloat16)


def fold_ninth(ninth_ref, out_ref):
    sources, width = ninth_ref.shape
    dims = (sources * SLOTS, sources)
    own = lax.shift_right_logical(iota(dims, 0), 3) == iota(dims, 1)
    place = jnp.bitwise_and(iota(dims, 0), SLOTS - 1)
    fold = jnp.concatenate([low(own & (place == r)) for r in range(SLOTS)], axis=1)
    folded = jnp.concatenate(
        [ninth_ref[:, r * EXTRA : (r + 1) * EXTRA] for r in range(SLOTS)], axis=0
    )
    out_ref[:, width:] = dot(fold, folded).astype(jnp.bfloat16)


def expert_kernel(
    rows_ref,
    cot_ref,
    gate_ref,
    up_ref,
    down_ref,
    back_ref,
    act_ref,
    rows_ninth,
    cot_ninth,
    gate_cot,
    up_cot,
    back_ninth,
):
    main = rows_ref.shape[0]
    sources = rows_ninth.shape[0]
    width = rows_ninth.shape[1]
    units = gate_ref.shape[1]
    unfold_ninth(rows_ref, rows_ninth)
    unfold_ninth(cot_ref, cot_ninth)
    block = 256

    def hidden_step(n, carry):
        cols = pl.ds(pl.multiple_of(n * block, block), block)
        gate_mat = gate_ref[:, cols]
        up_mat = up_ref[:, cols]
        down_mat = down_ref[cols, :]
        for rows, rows_in, cot_in in (
            (pl.ds(0, main), rows_ref[:, :width], cot_ref[:, :width]),
            (pl.ds(main, sources), rows_ninth[...], cot_ninth[...]),
        ):
            gate_act = dot(rows_in, gate_mat)
            up_act = dot(rows_in, up_mat)
            act_cot = dot(cot_in, down_mat, NT)
            sigma = 1.0 / (1.0 + jnp.exp(-gate_act))
            act = gate_act * sigma
            act_ref[rows, cols] = (act * up_act).astype(jnp.bfloat16)
            gate_cot[rows, cols] = (
                act_cot * up_act * sigma * (1.0 + gate_act * (1.0 - sigma))
            ).astype(jnp.bfloat16)
            up_cot[rows, cols] = (act_cot * act).astype(jnp.bfloat16)
        return carry

    lax.fori_loop(0, units // block, hidden_step, 0)

    def back_step(n, carry):
        cols = pl.ds(pl.multiple_of(n * block, block), block)
        gate_mat = gate_ref[cols, :]
        up_mat = up_ref[cols, :]
        back_ref[:, cols] = (
            dot(gate_cot[:main, :], gate_mat, NT) + dot(up_cot[:main, :], up_mat, NT)
        ).astype(jnp.bfloat16)
        back_ninth[:, cols] = (
            dot(gate_cot[main:, :], gate_mat, NT) + dot(up_cot[main:, :], up_mat, NT)
        ).astype(jnp.bfloat16)
        return carry

    lax.fori_loop(0, width // block, back_step, 0)
    fold_ninth(back_ninth, back_ref)


def produce_kernel(act_ref, down_ref, out_ref, out_ninth):
    main = out_ref.shape[0]
    width = out_ninth.shape[1]
    block = 256

    def step(n, carry):
        cols = pl.ds(pl.multiple_of(n * block, block), block)
        down_mat = down_ref[:, cols]
        out_ref[:, cols] = dot(act_ref[:main, :], down_mat).astype(jnp.bfloat16)
        out_ninth[:, cols] = dot(act_ref[main:, :], down_mat).astype(jnp.bfloat16)
        return carry

    lax.fori_loop(0, width // block, step, 0)
    fold_ninth(out_ninth, out_ref)


def residual_kernel(back_ref, slot_ref, hidden_ref, cot_ref, gain_ref, out_ref, normed_cot):
    tokens, width = hidden_ref.shape
    experts = slot_ref.shape[1]
    slot = dot(slot_ref[...].astype(jnp.bfloat16), low(repeat_lanes(experts)))
    place = jnp.bitwise_and(iota((tokens, experts * SLOTS), 1), SLOTS - 1)
    first = low(slot == place.astype(jnp.float32))
    ninth = slot == float(SLOTS)
    for c in range(width // EXTRA):
        cols = slice(c * EXTRA, (c + 1) * EXTRA)
        normed_cot[:, cols] = dot(first, back_ref[:, cols]) + dot(
            low(ninth & (place == c)), back_ref[:, width:]
        )
    hidden = hidden_ref[...].astype(jnp.float32)
    inverse = lax.rsqrt(jnp.mean(hidden * hidden, axis=1, keepdims=True) + EPSILON)
    gained = gain_ref[...] * normed_cot[...]
    mean = jnp.mean(hidden * gained, axis=1, keepdims=True)
    out_ref[...] = (
        cot_ref[...].astype(jnp.float32)
        + inverse * gained
        - hidden * (inverse * inverse * inverse * mean)
    ).astype(jnp.bfloat16)


def output_kernel(
    ret_ref, slot_ref, share_ref, chosen_ref, route_ref, hidden_ref, cot_ref, out_ref, route_out_ref
):
    tokens, width = hidden_ref.shape
    experts = slot_ref.shape[1]
    total = experts * SLOTS
    repeat = repeat_lanes(experts)
    slot = dot(slot_ref[...].astype(jnp.bfloat16), low(repeat))
    share = dot(share_ref[...], one(repeat), precision=HIGHEST)
    place = jnp.bitwise_and(iota((tokens, total), 1), SLOTS - 1)
    first = slot == place.astype(jnp.float32)
    ninth = slot == float(SLOTS)
    share_high = share.astype(jnp.bfloat16).astype(jnp.float32)
    share_rest = share - share_high

    def mix(mask, rows):
        return dot(jnp.where(mask, share_high, 0.0).astype(jnp.bfloat16), rows) + dot(
            jnp.where(mask, share_rest, 0.0).astype(jnp.bfloat16), rows
        )

    ninth_dots = jnp.zeros((tokens, total), jnp.float32)
    for c in range(width // EXTRA):
        cols = slice(c * EXTRA, (c + 1) * EXTRA)
        moe = mix(first, ret_ref[:, cols]) + mix(ninth & (place == c), ret_ref[:, width:])
        out_ref[:, cols] = (hidden_ref[:, cols].astype(jnp.float32) + moe).astype(jnp.bfloat16)
        ninth_dots = jnp.where(
            place == c, dot(cot_ref[:, cols], ret_ref[:, width:], NT), ninth_dots
        )
    dots = dot(cot_ref[...], ret_ref[:, :width], NT)
    picked = jnp.where(first, dots, jnp.where(ninth, ninth_dots, 0.0))
    owner = lax.shift_right_logical(iota((tokens, total), 1), 3)
    chosen = chosen_ref[...]
    route = route_ref[...]
    route_total = jnp.sum(route, axis=1, keepdims=True)
    route_share = route / route_total
    lanes = iota((tokens, TOPK), 1)
    route_dot = jnp.zeros((tokens, TOPK), jnp.float32)
    for k in range(TOPK):
        column = jnp.sum(
            jnp.where(owner == chosen[:, k : k + 1], picked, 0.0), axis=1, keepdims=True
        )
        route_dot = jnp.where(lanes == k, column, route_dot)
    route_out_ref[...] = (
        route_dot - jnp.sum(route_share * route_dot, axis=1, keepdims=True)
    ) / route_total


def heads_of(ref):
    return [ref[:, h * DH : (h + 1) * DH] for h in range(GROUP)]


def allowed_keys(index, begin, tokens):
    dims = (KEY_BLOCK, GROUP * tokens)
    return begin + iota(dims, 0) <= index * tokens + jnp.bitwise_and(iota(dims, 1), tokens - 1)


def forward_kernel(index_ref, q_ref, kv_ref, out_ref, log_ref, q_t):
    tokens = q_ref.shape[0]
    index = index_ref[0]
    for h, part in enumerate(heads_of(q_ref)):
        q_t[:, h * tokens : (h + 1) * tokens] = part.T

    def visit(block, state, masked):
        run_max, run_sum, acc = state
        begin = pl.multiple_of(block * KEY_BLOCK, KEY_BLOCK)
        keys = kv_ref[pl.ds(begin, KEY_BLOCK), :DH]
        values = kv_ref[pl.ds(begin, KEY_BLOCK), DH:]
        scores = dot(keys, q_t[...])
        if masked:
            scores = jnp.where(allowed_keys(index, begin, tokens), scores, NEG)
        new_max = jnp.maximum(run_max, jnp.max(scores, axis=0, keepdims=True))
        weights = jnp.exp2(scores * SCALE2 - new_max * SCALE2)
        keep = jnp.exp2((run_max - new_max) * SCALE2)
        run_sum = run_sum * keep + jnp.sum(weights, axis=0, keepdims=True)
        acc = acc * keep + dot(values.T, weights.astype(jnp.bfloat16))
        return new_max, run_sum, acc

    state = (
        jnp.full((1, GROUP * tokens), NEG, jnp.float32),
        jnp.zeros((1, GROUP * tokens), jnp.float32),
        jnp.zeros((DH, GROUP * tokens), jnp.float32),
    )
    full = (index * tokens) // KEY_BLOCK
    state = lax.fori_loop(0, full, lambda b, s: visit(b, s, False), state)
    run_max, run_sum, acc = visit(full, state, True)
    acc = acc / run_sum
    for h in range(GROUP):
        out_ref[:, h * DH : (h + 1) * DH] = (
            acc[:, h * tokens : (h + 1) * tokens].T.astype(jnp.bfloat16)
        )
    log_ref[0] = run_max * SCALE2 + jnp.log2(run_sum)


def backward_kernel(
    index_ref, q_ref, kv_ref, grad_ref, attended_ref, log_ref, dq_ref, dkv_ref, q_s, q_t, g_s, g_t, dq_acc
):
    tokens = q_ref.shape[0]
    index = index_ref[0]
    dots = []
    for h in range(GROUP):
        rows = slice(h * tokens, (h + 1) * tokens)
        cols = slice(h * DH, (h + 1) * DH)
        q_s[rows, :] = q_ref[:, cols]
        g_s[rows, :] = grad_ref[:, cols]
        q_t[:, rows] = q_ref[:, cols].T
        grad_t = grad_ref[:, cols].T
        g_t[:, rows] = grad_t
        dots.append(
            jnp.sum(
                grad_t.astype(jnp.float32) * attended_ref[:, cols].T.astype(jnp.float32),
                axis=0,
                keepdims=True,
            )
        )
    row_dot = jnp.concatenate(dots, axis=1)
    log_sum = log_ref[0]
    dq_acc[...] = jnp.zeros_like(dq_acc)

    def visit(block, masked):
        begin = pl.multiple_of(block * KEY_BLOCK, KEY_BLOCK)
        keys = kv_ref[pl.ds(begin, KEY_BLOCK), :DH]
        values = kv_ref[pl.ds(begin, KEY_BLOCK), DH:]
        weights = jnp.exp2(dot(keys, q_t[...]) * SCALE2 - log_sum)
        if masked:
            weights = jnp.where(allowed_keys(index, begin, tokens), weights, 0.0)
        cot = (weights * (dot(values, g_t[...]) - row_dot)).astype(jnp.bfloat16)
        dkv_ref[pl.ds(begin, KEY_BLOCK), DH:] = dot(weights.astype(jnp.bfloat16), g_s[...]).astype(
            jnp.bfloat16
        )
        dkv_ref[pl.ds(begin, KEY_BLOCK), :DH] = (dot(cot, q_s[...]) * SCALE).astype(jnp.bfloat16)
        dq_acc[...] += dot(keys.T, cot)

    full = (index * tokens) // KEY_BLOCK

    def step(block, carry):
        visit(block, False)
        return carry

    lax.fori_loop(0, full, step, 0)
    visit(full, True)
    for h in range(GROUP):
        dq_ref[:, h * DH : (h + 1) * DH] = (
            (dq_acc[:, h * tokens : (h + 1) * tokens] * SCALE).T.astype(jnp.bfloat16)
        )


def attend_forward(index, query, kv):
    tokens, width = query.shape
    seq = kv.shape[0]
    return call(
        forward_kernel,
        (shape((tokens, width), jnp.bfloat16), shape((KVH, 1, GROUP * tokens), jnp.float32)),
        (index, query, kv),
        flops=4 * tokens * seq * width,
        grid_spec=pltpu.PrefetchScalarGridSpec(
            num_scalar_prefetch=1,
            grid=(KVH,),
            in_specs=[
                pl.BlockSpec((tokens, GQ), lambda g, i: (0, g)),
                pl.BlockSpec((seq, 2 * DH), lambda g, i: (0, g)),
            ],
            out_specs=[
                pl.BlockSpec((tokens, GQ), lambda g, i: (0, g)),
                pl.BlockSpec((1, 1, GROUP * tokens), lambda g, i: (g, 0, 0)),
            ],
            scratch_shapes=[pltpu.VMEM((DH, GROUP * tokens), jnp.bfloat16)],
        ),
    )


def attend_backward(index, query, kv, grad, attended, log_sum):
    tokens, width = query.shape
    seq = kv.shape[0]
    rows = pl.BlockSpec((tokens, GQ), lambda g, i: (0, g))
    pairs = pl.BlockSpec((seq, 2 * DH), lambda g, i: (0, g))
    return call(
        backward_kernel,
        (shape((tokens, width), jnp.bfloat16), shape((seq, KVH * 2 * DH), jnp.bfloat16)),
        (index, query, kv, grad, attended, log_sum),
        flops=10 * tokens * seq * width,
        grid_spec=pltpu.PrefetchScalarGridSpec(
            num_scalar_prefetch=1,
            grid=(KVH,),
            in_specs=[
                rows,
                pairs,
                rows,
                rows,
                pl.BlockSpec((1, 1, GROUP * tokens), lambda g, i: (g, 0, 0)),
            ],
            out_specs=[rows, pairs],
            scratch_shapes=[
                pltpu.VMEM((GROUP * tokens, DH), jnp.bfloat16),
                pltpu.VMEM((DH, GROUP * tokens), jnp.bfloat16),
                pltpu.VMEM((GROUP * tokens, DH), jnp.bfloat16),
                pltpu.VMEM((DH, GROUP * tokens), jnp.bfloat16),
                pltpu.VMEM((DH, GROUP * tokens), jnp.float32),
            ],
        ),
    )


def pair_heads(key_rows, value_rows):
    parts = []
    for g in range(KVH):
        parts += [key_rows[:, g * DH : (g + 1) * DH], value_rows[:, g * DH : (g + 1) * DH]]
    return jnp.concatenate(parts, axis=1)


def exchange(rows, axes):
    return lax.all_to_all(rows, axes, split_axis=0, concat_axis=0, tiled=True)


def per_device(
    residual,
    query_heads,
    key_heads,
    value_heads,
    norm_gain,
    chosen_experts,
    route_weights,
    gate_weight,
    up_weight,
    down_weight,
    cotangent,
):
    bf16, f32 = jnp.bfloat16, jnp.float32
    tokens, width = residual.shape[1:]
    ctx_count = lax.axis_size("ctx")
    experts = ctx_count * lax.axis_size("exp")
    seq = tokens * ctx_count
    ctx_index = lax.axis_index("ctx")
    index = ctx_index.reshape(1).astype(jnp.int32)
    slots = experts * SLOTS
    wide = width + EXTRA
    units = gate_weight.shape[2]
    residual, query, cot = residual[0], query_heads[0], cotangent[0]
    chosen, route = chosen_experts[0], route_weights[0]
    gain = norm_gain[None]
    gate_mat, up_mat, down_mat = gate_weight[0], up_weight[0], down_weight[0]

    def to_devices(rows):
        return exchange(rows.reshape(experts, SLOTS, wide), ("ctx", "exp")).reshape(slots, wide)

    pair = pair_heads(key_heads[0], value_heads[0])
    kv = exchange(jnp.broadcast_to(pair[None], (ctx_count,) + pair.shape), "ctx")
    kv = kv.reshape(seq, 2 * KVH * DH)

    send_cot, slot, slot_t, share = call(
        send_cot_kernel,
        (
            shape((slots, wide), bf16),
            shape((tokens, experts), f32),
            shape((experts, tokens), f32),
            shape((tokens, experts), f32),
        ),
        (chosen, route, cot),
        flops=2 * slots * tokens * width,
    )
    send_cot, kv = lax.optimization_barrier((send_cot, kv))
    cot_in = to_devices(send_cot)
    attended, log_sum = attend_forward(index, query, kv)
    send_normed, hidden, normed = call(
        send_normed_kernel,
        (shape((slots, wide), bf16), shape((tokens, width), bf16), shape((tokens, width), bf16)),
        (residual, attended, gain, slot_t),
        flops=2 * slots * tokens * width,
    )
    incoming = to_devices(send_normed)

    row_cot, activation = call(
        expert_kernel,
        (shape((slots, wide), bf16), shape((slots + experts, units), bf16)),
        (incoming, cot_in, gate_mat, up_mat, down_mat),
        flops=10 * (slots + experts) * width * units,
        scratch_shapes=[
            pltpu.VMEM((experts, width), bf16),
            pltpu.VMEM((experts, width), bf16),
            pltpu.VMEM((slots + experts, units), bf16),
            pltpu.VMEM((slots + experts, units), bf16),
            pltpu.VMEM((experts, width), bf16),
        ],
    )
    cot_back = to_devices(row_cot)
    produced = call(
        produce_kernel,
        shape((slots, wide), bf16),
        (activation, down_mat),
        flops=2 * (slots + experts) * width * units,
        scratch_shapes=[pltpu.VMEM((experts, width), bf16)],
    )
    produced, cot_back = lax.optimization_barrier((produced, cot_back))
    returned = to_devices(produced)
    residual_gradient = call(
        residual_kernel,
        shape((tokens, width), bf16),
        (cot_back, slot, hidden, cot, gain),
        flops=2 * slots * tokens * width,
        scratch_shapes=[pltpu.VMEM((tokens, width), f32)],
    )
    query_gradient, pair_terms = attend_backward(
        index, query, kv, residual_gradient, attended, log_sum
    )
    pair_terms = exchange(pair_terms.reshape(ctx_count, tokens, 2 * KVH * DH), "ctx")
    counted = (jnp.arange(ctx_count, dtype=jnp.int32) >= ctx_index)[:, None, None]
    pair_sum = jnp.sum(jnp.where(counted, pair_terms.astype(f32), 0.0), axis=0).astype(bf16)
    layer_out, route_gradient = call(
        output_kernel,
        (shape((tokens, width), bf16), shape((tokens, TOPK), f32)),
        (returned, slot, share, chosen, route, hidden, cot),
        flops=6 * slots * tokens * width,
    )
    halves = [pair_sum[:, n * DH : (n + 1) * DH] for n in range(2 * KVH)]
    key_gradient = jnp.concatenate(halves[0::2], axis=1)
    value_gradient = jnp.concatenate(halves[1::2], axis=1)
    return (
        layer_out[None],
        residual_gradient[None],
        query_gradient[None],
        key_gradient[None],
        value_gradient[None],
        route_gradient[None],
    )


def solution(mesh):
    rows = P("exp", "ctx", None)
    weights = P(("ctx", "exp"), None, None)
    in_specs = (rows, rows, rows, rows, P(), rows, rows, weights, weights, weights, rows)
    return jax.shard_map(
        per_device, mesh=mesh, in_specs=in_specs, out_specs=(rows,) * 6, check_vma=False
    )
```

time: 1250 us -> 499 us (0.40)
  waiting for transfers between devices: 834 us -> 149 us
  blocking collectives: 0 us -> 234 us
  matrix products: 157 us -> 0 us
  local copies, waits for them, and re-layouts: 124 us -> 6.28 us
  Pallas kernels: 0 us -> 79.2 us
  other arithmetic: 70.5 us -> 4.52 us
  starting transfers between devices: 42 us -> 23.1 us
  between operations: 16.2 us -> 0.71 us
    all_gather x2 -> x0, waiting for transfers between devices: 300 us -> none  [the longest x1 174 us: over_keys(): lax.all_gather(key_local, 'ctx', axis=0, tiled=True)]
    reduce_scatter x2 -> x0, waiting for transfers between devices: 236 us -> none  [the longest x1 163 us: per_device(): lax.psum_scatter(value_total.astype(jnp.bfloat16), 'ctx', scatter_dimensi...]
    all_to_all x0 -> x3, blocking collectives: none -> 234 us  [exchange(): return lax.all_to_all(rows, axes, split_axis=0, concat_axis=0, tiled=True)]
    dot_general x20 -> x0, matrix products: 157 us -> none  [the longest x2 25.8 us: backward_tile(): jnp.einsum('kgij,ikgd->jkd', weights.astype(jnp.bfloat16), grad_half, pre...]
    all_to_all x4 -> x3, waiting for transfers between devices: 297 us -> 149 us  [exchange(): return lax.all_to_all(rows, axes, split_axis=0, concat_axis=0, tiled=True)]
    pallas_call x0 -> x8, Pallas kernels: none -> 79.2 us  [call(): pl.pallas_call(kernel, out_shape=out_shape, compiler_params=pltpu.Compile...]
    reshape x8 -> x0, local copies, waits for them, and re-layouts: 66.3 us -> none  [the longest x2 16.3 us: spread(): return filled.reshape(expert_count, capacity, width)]
    reduce_sum x9 -> x1, other arithmetic: 31.8 us -> 3.22 us  [per_device(): jnp.sum(jnp.where(counted, pair_terms.astype(f32), 0.0), axis=0)]
  transfers between devices with their start and end apart: 8 -> 3, of which waited for: 7 -> 3; matrix products, arithmetic and copies ran while one was open for 15% -> 1% of each run, Pallas kernels for 0% -> 3%
where the time goes in v1:
time: 499 us; the launch traced here: 497 us
  blocking collectives  234 us (47%)
  waiting for transfers between devices  149 us (30%)
  Pallas kernels  79.2 us (16%)
  starting transfers between devices  23.1 us (5%)
  local copies, waits for them, and re-layouts  6.28 us (1%)
    all_to_all x3, blocking collectives, exchange(): return lax.all_to_all(rows, axes, split_axis=0, concat_axis=0, tiled=True)  234 us
    all_to_all x3, waiting for transfers between devices, exchange(): return lax.all_to_all(rows, axes, split_axis=0, concat_axis=0, tiled=True)  149 us
    pallas_call x8, Pallas kernels, call(): pl.pallas_call(kernel, out_shape=out_shape, compiler_params=pltpu.Compile...  79.2 us
    all_to_all x3, starting transfers between devices, exchange(): return lax.all_to_all(rows, axes, split_axis=0, concat_axis=0, tiled=True)  23.1 us
  transfers between devices with their start and end apart: 3, of which 3 were waited for; matrix products, arithmetic and copies ran while one was open for 1% of the time, Pallas kernels for 3%

profile of v1, /device:TPU:0, one launch (start us, length us, event | category | flops | bytes accessed | tf_op | source)
XLA Modules:
  0.0 497.0 jit_solution(16313648321757630619)
XLA Ops:
  0.6 0.8 fusion.1
  1.5 2.5 broadcast_in_dim.40
  4.0 0.0 copy-start
  4.0 0.0 copy-start.1
  4.0 9.5 %all-to-all-start = ((bf16[32,128,512]{2,1,0:T(8,128)(2,1)}), bf16[32,128,512]{2,1,0:T(8,128)(2,1)}, u32[]{:S(2)}, u32[]{:S(2)}) async-start(bf16[32,128,512]{2,1,0:T(8,128)(2,1)} %broadcast_in_dim.40), calls=%async_computation | async-start | bytes 8388608 | tf_op jit(solution)/shard_map/all_to_all | solution.py:470
  13.5 0.0 copy-done
  13.5 0.7 copy.17
  14.2 0.0 copy-done.1
  14.2 0.7 copy.18
  15.0 6.4 %shard_map.154 = (bf16[1024,2304]{1,0:T(8,128)(2,1)}, f32[128,128]{1,0:T(8,128)}, f32[128,128]{1,0:T(8,128)}, f32[128,128]{1,0:T(8,128)}) custom-call(s32[128,8]{1,0:T(8,128)} %bitcast.43, f32[128,8]{1,0:T(8,128)} %bitcast.45, bf16[128,2048]{1,0:T(8,128)(2,1)} %bitcast.39), custom_call_target="tpu_custom_call" | custom-call | flops 536870912 | bytes 5447680 | tf_op jit(solution)/shard_map/pallas_call | solution.py:44
  21.3 47.2 %all-to-all-done = bf16[32,128,512]{2,1,0:T(8,128)(2,1)} async-done(((bf16[32,128,512]{2,1,0:T(8,128)(2,1)}), bf16[32,128,512]{2,1,0:T(8,128)(2,1)}, u32[]{:S(2)}, u32[]{:S(2)}) %all-to-all-start) | async-done | bytes 4194336 | tf_op jit(solution)/shard_map/all_to_all | solution.py:470
  68.5 4.2 shard_map.155
  72.8 0.0 slice-start
  72.8 5.8 %shard_map.156 = (bf16[1024,2304]{1,0:T(8,128)(2,1)}, bf16[128,2048]{1,0:T(8,128)(2,1)}, bf16[128,2048]{1,0:T(8,128)(2,1)}) custom-call(bf16[128,2048]{1,0:T(8,128)(2,1)} %bitcast.56, bf16[128,2048]{1,0:T(8,128)(2,1)} %get-tuple-element.26.attended_ref, f32[1,2048]{1,0:T(1,128)} %bitcast.50, f32[128,128]{1,0:T(8,128)} %get-tuple-element.27.slot_t_ref), custom_call_target="tpu_custom_call" | custom-call | flops 536870912 | bytes 6889472 | tf_op jit(solution)/shard_map/pallas_call | solution.py:44
  78.5 0.0 slice-start.1
  78.5 88.4 %all_to_all.30 = bf16[128,8,2304]{2,1,0:T(8,128)(2,1)} all-to-all(bf16[128,8,2304]{2,1,0:T(8,128)(2,1)} %bitcast.36), channel_id=1, replica_groups=mesh['ctx'=32,'exp'=4] {'ctx','exp'}, dimensions={0} | all-to-all | bytes 9437184 | tf_op jit(solution)/shard_map/all_to_all | solution.py:470
  166.9 0.0 slice-done
  166.9 0.0 slice-done.1
  166.9 65.4 %all_to_all.31 = bf16[128,8,2304]{2,1,0:T(8,128)(2,1)} all-to-all(bf16[128,8,2304]{2,1,0:T(8,128)(2,1)S(1)} %bitcast.33), channel_id=1, replica_groups=mesh['ctx'=32,'exp'=4] {'ctx','exp'}, dimensions={0} | all-to-all | bytes 9437184 | tf_op jit(solution)/shard_map/all_to_all | solution.py:470
  232.4 32.7 %shard_map.157 = (bf16[1024,2304]{1,0:T(8,128)(2,1)}, bf16[1152,768]{1,0:T(8,128)(2,1)}) custom-call(bf16[1024,2304]{1,0:T(8,128)(2,1)} %bitcast.35, bf16[1024,2304]{1,0:T(8,128)(2,1)} %bitcast.37, bf16[2048,768]{1,0:T(8,128)(2,1)} %bitcast.52, bf16[2048,768]{1,0:T(8,128)(2,1)} %bitcast.53, bf16[768,2048]{1,0:T(8,128)(2,1)} %bitcast.54), custom_call_target="tpu_custom_call" | custom-call | flops 18119393280 | bytes 25362432 | tf_op jit(solution)/shard_map/pallas_call | solution.py:44
  265.1 6.8 %all-to-all-start.3 = ((bf16[128,8,2304]{2,1,0:T(8,128)(2,1)}), bf16[128,8,2304]{2,1,0:T(8,128)(2,1)}, u32[]{:S(2)}, u32[]{:S(2)}) async-start(bf16[128,8,2304]{2,1,0:T(8,128)(2,1)} %bitcast.34), calls=%async_computation.3 | async-start | bytes 9437184 | tf_op jit(solution)/shard_map/all_to_all | solution.py:470
  271.9 10.4 %shard_map.158 = bf16[1024,2304]{1,0:T(8,128)(2,1)} custom-call(bf16[1152,768]{1,0:T(8,128)(2,1)} %get-tuple-element.30.act_ref, bf16[768,2048]{1,0:T(8,128)(2,1)} %bitcast.55), custom_call_target="tpu_custom_call" | custom-call | flops 3623878656 | bytes 9633792 | tf_op jit(solution)/shard_map/pallas_call | solution.py:44
  282.3 48.0 %all-to-all-done.3 = bf16[128,8,2304]{2,1,0:T(8,128)(2,1)} async-done(((bf16[128,8,2304]{2,1,0:T(8,128)(2,1)}), bf16[128,8,2304]{2,1,0:T(8,128)(2,1)}, u32[]{:S(2)}, u32[]{:S(2)}) %all-to-all-start.3) | async-done | bytes 4718624 | tf_op jit(solution)/shard_map/all_to_all | solution.py:470
  330.3 5.0 %shard_map.160.grad_ref = bf16[128,2048]{1,0:T(8,128)(2,1)} custom-call(bf16[1024,2304]{1,0:T(8,128)(2,1)} %bitcast.18.back_ref, f32[128,128]{1,0:T(8,128)} %get-tuple-element.33.slot_ref, bf16[128,2048]{1,0:T(8,128)(2,1)} %get-tuple-element.35.hidden_ref, bf16[128,2048]{1,0:T(8,128)(2,1)} %bitcast.40, f32[1,2048]{1,0:T(1,128)} %bitcast.51), custom_call_target="tpu_custom_call" | custom-call | flops 536870912 | bytes 6365184 | tf_op jit(solution)/shard_map/pallas_call | solution.py:44
  335.2 5.6 %shard_map.161 = (bf16[128,2048]{1,0:T(8,128)(2,1)}, bf16[4096,512]{1,0:T(8,128)(2,1)}) custom-call(s32[1]{0:T(128)} %bitcast.1.index_ref, bf16[128,2048]{1,0:T(8,128)(2,1)} %bitcast.58, bf16[4096,512]{1,0:T(8,128)(2,1)} %bitcast.8.kv_ref, bf16[128,2048]{1,0:T(8,128)(2,1)} %shard_map.160.grad_ref, bf16[128,2048]{1,0:T(8,128)(2,1)} %get-tuple-element.26.attended_ref, ...), custom_call_target="tpu_custom_call" | custom-call | flops 10737418240 | bytes 10493956 | tf_op jit(solution)/shard_map/pallas_call | solution.py:44
  340.9 80.5 %all_to_all.32 = bf16[32,128,512]{2,1,0:T(8,128)(2,1)} all-to-all(bf16[32,128,512]{2,1,0:T(8,128)(2,1)} %bitcast.38), channel_id=1, replica_groups=mesh['ctx'=32,'exp'=4] {'ctx'}, dimensions={0} | all-to-all | bytes 8388608 | tf_op jit(solution)/shard_map/all_to_all | solution.py:470
  421.3 6.8 %all-to-all-start.4 = ((bf16[128,8,2304]{2,1,0:T(8,128)(2,1)}), bf16[128,8,2304]{2,1,0:T(8,128)(2,1)}, u32[]{:S(2)}, u32[]{:S(2)}) async-start(bf16[128,8,2304]{2,1,0:T(8,128)(2,1)} %bitcast.30), calls=%async_computation.4 | async-start | bytes 9437184 | tf_op jit(solution)/shard_map/all_to_all | solution.py:470
  428.2 3.2 select_reduce_fusion
  431.4 0.6 maximum_bitcast_fusion.1
  432.1 0.6 maximum_bitcast_fusion
  432.7 53.6 %all-to-all-done.4 = bf16[128,8,2304]{2,1,0:T(8,128)(2,1)} async-done(((bf16[128,8,2304]{2,1,0:T(8,128)(2,1)}), bf16[128,8,2304]{2,1,0:T(8,128)(2,1)}, u32[]{:S(2)}, u32[]{:S(2)}) %all-to-all-start.4) | async-done | bytes 4718624 | tf_op jit(solution)/shard_map/all_to_all | solution.py:470
  486.3 9.1 %shard_map.159 = (bf16[128,2048]{1,0:T(8,128)(2,1)}, f32[128,8]{1,0:T(8,128)}) custom-call(bf16[1024,2304]{1,0:T(8,128)(2,1)} %bitcast.20.ret_ref, f32[128,128]{1,0:T(8,128)} %get-tuple-element.33.slot_ref, f32[128,128]{1,0:T(8,128)} %get-tuple-element.34.share_ref, s32[128,8]{1,0:T(8,128)} %bitcast.44, f32[128,8]{1,0:T(8,128)} %bitcast.46, ...), custom_call_target="tpu_custom_call" | custom-call | flops 1610612736 | bytes 6434816 | tf_op jit(solution)/shard_map/pallas_call | solution.py:44
  495.5 1.5 copy.19
  (4 shorter events, 0.1 us)
Async XLA Ops:
  4.0 9.5 %copy-start = (s32[1,128,8]{1,2,0:T(8,128)S(1)}, s32[1,128,8]{1,2,0:T(8,128)}, u32[]{:S(2)}) copy-start(s32[1,128,8]{1,2,0:T(8,128)} %param.16) | copy-start | bytes 12292
  4.0 10.3 %copy-start.1 = (f32[1,128,8]{1,2,0:T(8,128)S(1)}, f32[1,128,8]{1,2,0:T(8,128)}, u32[]{:S(2)}) copy-start(f32[1,128,8]{1,2,0:T(8,128)} %param.17) | copy-start | bytes 12292
  4.0 64.5 %all-to-all-start = ((bf16[32,128,512]{2,1,0:T(8,128)(2,1)}), bf16[32,128,512]{2,1,0:T(8,128)(2,1)}, u32[]{:S(2)}, u32[]{:S(2)}) async-start(bf16[32,128,512]{2,1,0:T(8,128)(2,1)} %broadcast_in_dim.40), calls=%async_computation | async-start | bytes 8388608 | tf_op jit(solution)/shard_map/all_to_all | solution.py:470
  72.8 94.2 %slice-start = ((s8[4718592]{0:T(1024)(128)(4,1)}), s8[524288]{0:T(1024)(128)(4,1)S(1)}, s32[]{:S(2)}) async-start(s8[4718592]{0:T(1024)(128)(4,1)} %bitcast.31), calls=%async_computation.6 | async-start | bytes 1048576
  78.5 88.4 %slice-start.1 = ((s8[4718592]{0:T(1024)(128)(4,1)}), s8[4194304]{0:T(1024)(128)(4,1)S(1)}, s32[]{:S(2)}) async-start(s8[4718592]{0:T(1024)(128)(4,1)} %bitcast.31), calls=%async_computation.7 | async-start | bytes 8388608
  265.1 65.2 %all-to-all-start.3 = ((bf16[128,8,2304]{2,1,0:T(8,128)(2,1)}), bf16[128,8,2304]{2,1,0:T(8,128)(2,1)}, u32[]{:S(2)}, u32[]{:S(2)}) async-start(bf16[128,8,2304]{2,1,0:T(8,128)(2,1)} %bitcast.34), calls=%async_computation.3 | async-start | bytes 9437184 | tf_op jit(solution)/shard_map/all_to_all | solution.py:470
  421.3 65.0 %all-to-all-start.4 = ((bf16[128,8,2304]{2,1,0:T(8,128)(2,1)}), bf16[128,8,2304]{2,1,0:T(8,128)(2,1)}, u32[]{:S(2)}, u32[]{:S(2)}) async-start(bf16[128,8,2304]{2,1,0:T(8,128)(2,1)} %bitcast.30), calls=%async_computation.4 | async-start | bytes 9437184 | tf_op jit(solution)/shard_map/all_to_all | solution.py:470
